TPU v7x, 128 devices: a whole 4x4x4 slice. The times are simulated.
128 devices in a mesh: segment: 2 (over z_hi), row: 8 (over y, core), col: 8 (over x, z_lo).
Axes of the slice: x: 4, y: 4, z: 4 (z_hi: 2, z_lo: 2; z = z_hi * 2 + z_lo), core: 2. Of those that a mesh axis runs over, the one named last changes fastest.
Arguments:
- dosage: float32 [2048, 12288], P(('segment', 'col'), 'row'), may hold values from 0 to 2, as said below
- missing: int32 [2048, 12288], P(('segment', 'col'), 'row'), may hold values 0 or 1
- residuals: bfloat16 [12288, 256], P('row'), may hold values from -6 to 6
- global_grm: bfloat16 [12288, 12288], P('row', 'col'), may hold values from -1 to 2
- seg_counts: int32 [6], replicated, may hold values from 1 to 1024, 2048 in all
Outputs:
- scores: bfloat16 [6, 12288, 256], P(None, ('row', 'col'), 'segment')
Inputs may be any that keep to these rules, and one draw needn't show every extreme that they name: `dosage`: imputed alternative-allele dosages. 1 marks a missing genotype. `seg_counts`: SNP counts of the 6 segments, laid end to end over the 2048 variants; they sum to 2048 and the largest is exactly 1024.
All inputs are finite; a program needn't handle non-finite values. No bound on the sum of `missing` on one device may be relied on, other than what follows from the above.
Results may differ from a plain program's by a relative error of at most 0.0053.
Values may be sent and summed in bfloat16 or wider, within the bound.
A program may use at most 320 MiB of HBM per device.

v0:
```python
import jax
import jax.numpy as jnp
from jax import lax
from jax.sharding import PartitionSpec as P

MOST = 1024
BLOCK = 256


def broadcast(shard, axis, root):
    mine = lax.axis_index(axis) == root
    return lax.psum(jnp.where(mine, shard, jnp.zeros_like(shard)), axis)


def gram_update(total, row_geno, col_geno, lower, upper, block_num):
    variants = row_geno.shape[0]
    nominal = lower + block_num * BLOCK
    first_row = jnp.minimum(nominal, variants - BLOCK)
    left_block = lax.dynamic_slice_in_dim(row_geno, first_row, BLOCK, 0)
    right_block = lax.dynamic_slice_in_dim(col_geno, first_row, BLOCK, 0)
    var_index = first_row + jnp.arange(BLOCK, dtype=jnp.int32)
    keep_mask = (var_index >= nominal) & (var_index < upper)
    left_block = jnp.where(keep_mask[:, None], left_block, jnp.zeros_like(left_block))
    return total + lax.dot_general(
        left_block, right_block, (((0,), (0,)), ((), ())), preferred_element_type=jnp.float32
    )


def segment_gram(row_geno, col_geno, lower, upper):
    local_gram = jnp.zeros((row_geno.shape[1], col_geno.shape[1]), jnp.float32)
    for block_num in range(MOST // BLOCK):

        def with_block(carry, block_num=block_num):
            return gram_update(carry, row_geno, col_geno, lower, upper, block_num)

        def without_block(carry):
            return carry

        local_gram = lax.cond(
            upper - lower > block_num * BLOCK, with_block, without_block, local_gram
        )
    return local_gram


def make_hadamard(local_gram, seg_count, global_grm):
    return (local_gram / seg_count.astype(jnp.float32) * global_grm).astype(jnp.bfloat16)


def shards(dosage, missing, residuals, global_grm, seg_counts):
    observed = (1 - missing).astype(jnp.float32)
    alt_local = jnp.sum(dosage * observed, axis=1)
    obs_local = jnp.sum(observed, axis=1)
    alt_total, obs_total = lax.psum((alt_local, obs_local), "row")
    allele_freq = (alt_total + 1.0) / (2.0 * obs_total + 2.0)
    allele_spread = jnp.sqrt(2.0 * allele_freq * (1.0 - allele_freq))
    standard = (observed * (dosage - 2.0 * allele_freq[:, None]) / allele_spread[:, None]).astype(
        jnp.bfloat16
    )
    group_id = lax.axis_index("segment")
    group_count = lax.axis_size("segment")
    col_count = lax.axis_size("col")
    segments = seg_counts.shape[0]
    seg_starts = jnp.cumsum(seg_counts) - seg_counts
    tile_size = standard.shape[1]
    dev_rows = tile_size // col_count
    half_cols = residuals.shape[1] // group_count
    row_geno = lax.all_gather(standard, "col", axis=0, tiled=True)
    col_geno, col_res = (
        broadcast(row_geno, "row", lax.axis_index("col")),
        broadcast(residuals, "row", lax.axis_index("col")),
    )
    half_vars = row_geno.shape[0]
    lower_bound = group_id * half_vars
    hadamards = []
    for segment_num in range(segments):
        seg_count = seg_counts[segment_num]
        seg_start = seg_starts[segment_num]
        lower = jnp.clip(seg_start - lower_bound, 0, half_vars)
        upper = jnp.clip(seg_start + seg_count - lower_bound, 0, half_vars)
        hadamards.append(
            make_hadamard(segment_gram(row_geno, col_geno, lower, upper), seg_count, global_grm)
        )

    def one_piece(piece_num):
        half_num = piece_num // col_count
        block_num = piece_num % col_count
        res_half = lax.dynamic_slice_in_dim(col_res, half_num * half_cols, half_cols, 1)
        return jnp.concatenate(
            [
                jnp.dot(
                    lax.dynamic_slice_in_dim(hadamard, block_num * dev_rows, dev_rows, 0),
                    res_half,
                    preferred_element_type=jnp.float32,
                )
                for hadamard in hadamards
            ],
            axis=1,
        )

    stacked = lax.map(
        one_piece,
        jnp.arange(lax.axis_size(("segment", "col")) * dev_rows // dev_rows, dtype=jnp.int32),
    )
    summed = lax.psum_scatter(
        stacked.reshape(lax.axis_size(("segment", "col")) * dev_rows, segments * half_cols),
        ("segment", "col"),
        scatter_dimension=0,
        tiled=True,
    )
    scores = summed.reshape(dev_rows, segments, half_cols).transpose(1, 0, 2)
    return scores.astype(jnp.bfloat16)


def solution(mesh):
    placed = (
        P(("segment", "col"), "row"),
        P(("segment", "col"), "row"),
        P("row", None),
        P("row", "col"),
        P(),
    )
    return jax.shard_map(
        shards,
        mesh=mesh,
        in_specs=placed,
        out_specs=P(None, ("row", "col"), "segment"),
        check_vma=False,
    )
```

profile of v0, /device:TPU:3, one launch (start us, length us, event | category | flops | bytes accessed | tf_op | source)
XLA Modules:
  0.0 668.0 jit_solution(17789371256403038519)
XLA Ops:
  6.5 1.6 multiply_reduce_fusion
  8.1 12.6 %all-reduce = (f32[128]{0:T(128)S(1)}, f32[128]{0:T(128)S(1)}) all-reduce(f32[128]{0:T(128)S(1)} %get-tuple-element.567, f32[128]{0:T(128)S(1)} %get-tuple-element.566), channel_id=1, replica_groups=mesh['segment'=2,'row'=8,'col'=8] {'row'}, use_global_device_ids=true, to_apply=%region_5.6 | all-reduce | flops 256 | bytes 2048 | tf_op jit(solution)/shard_map/psum | solution.py:53
  20.8 2.3 divide_convert_fusion
  24.1 71.0 %all-gather.2.cloned.1.call-done = bf16[1024,1536]{1,0:T(8,128)(2,1)} async-done(((bf16[128,1536]{1,0:T(8,128)(2,1)}), bf16[1024,1536]{1,0:T(8,128)(2,1)}) %all-gather.2.cloned.1.call-update) | async-done | bytes 3145744 | tf_op jit(solution)/shard_map/all_gather | solution.py:67
  95.1 1.8 broadcast_select_fusion
  114.0 56.4 %all-reduce.4.cloned.1.call-done = (bf16[1024,1536]{1,0:T(8,128)(2,1)}, bf16[1536,256]{1,0:T(8,128)(2,1)}) async-done(((bf16[1024,1536]{1,0:T(8,128)(2,1)}, bf16[1536,256]{1,0:T(8,128)(2,1)}), (bf16[1024,1536]{1,0:T(8,128)(2,1)}, bf16[1536,256]{1,0:T(8,128)(2,1)})) %all-reduce.4.cloned.1.call-update) | async-done | bytes 3932176 | tf_op jit(solution)/shard_map/psum | solution.py:12
  170.4 6.4 conditional.24
  170.4 6.4 fusion
  176.8 9.2 %conditional.25 = (f32[1536,1536]{1,0:T(8,128)}) conditional(s32[]{:T(128)} %convert_element_type.133, f32[1536,1536]{1,0:T(8,128)} %get-tuple-element.735, (s32[]{:T(128)}, s32[]{:T(128)}, bf16[1024,1536]{1,0:T(8,128)(2,1)S(1)}, bf16[1024,1536]{1,0:T(8,128)(2,1)}, f32[1536,1536]{1,0:T(8,128)}) %tuple.277), branch_computations={%region_9.10_spmd, %region_10.11_spmd} | conditional | flops 1210713088 | bytes 20449102 | solution.py:39
  176.8 9.2 %convolution_add_fusion = f32[1536,1536]{1,0:T(8,128)} fusion(f32[1536,1536]{1,0:T(8,128)} %get-tuple-element.443, bf16[1024,1536]{1,0:T(8,128)(2,1)} %get-tuple-element.447, s32[]{:T(128)S(6)} %select_n.167, bf16[1024,1536]{1,0:T(8,128)(2,1)S(1)} %get-tuple-element.446, pred[256]{0:T(512)(128)(4,1)S(1)} %compare_and_fusion.1), kind=kOutput, calls=%fused_computation.9 | convolution fusion | flops 1210712064 | bytes 20448768 | tf_op jit(solution)/shard_map/cond/branch_1_fun/dot_general | solution.py:24
  186.0 4.7 conditional.40
  186.0 4.7 broadcast.377
  191.2 4.9 conditional.36
  191.2 4.9 broadcast.372
  196.1 2.9 conditional.39
  198.9 4.9 conditional.32
  198.9 4.9 broadcast.367
  203.8 6.4 conditional.28
  203.8 6.3 fusion.29
  210.2 9.4 %conditional.29 = (f32[1536,1536]{1,0:T(8,128)}) conditional(s32[]{:T(128)} %convert_element_type.142, f32[1536,1536]{1,0:T(8,128)} %get-tuple-element.739, (s32[]{:T(128)}, s32[]{:T(128)}, bf16[1024,1536]{1,0:T(8,128)(2,1)S(1)}, bf16[1024,1536]{1,0:T(8,128)(2,1)}, f32[1536,1536]{1,0:T(8,128)}) %tuple.293), branch_computations={%region_17.18_spmd, %region_18.19_spmd} | conditional | flops 1210713088 | bytes 20449102 | solution.py:39
  210.4 9.2 %convolution_add_fusion.3 = f32[1536,1536]{1,0:T(8,128)} fusion(f32[1536,1536]{1,0:T(8,128)} %get-tuple-element.462, bf16[1024,1536]{1,0:T(8,128)(2,1)} %get-tuple-element.466, s32[]{:T(128)S(6)} %select_n.175, bf16[1024,1536]{1,0:T(8,128)(2,1)S(1)} %get-tuple-element.465, pred[256]{0:T(512)(128)(4,1)S(1)} %compare_and_fusion.5), kind=kOutput, calls=%fused_computation.45 | convolution fusion | flops 1210712064 | bytes 20448768 | tf_op jit(solution)/shard_map/cond/branch_1_fun/dot_general | solution.py:24
  219.6 9.2 %conditional.30 = (f32[1536,1536]{1,0:T(8,128)}) conditional(s32[]{:T(128)} %convert_element_type.141, f32[1536,1536]{1,0:T(8,128)} %get-tuple-element.740, (s32[]{:T(128)}, s32[]{:T(128)}, bf16[1024,1536]{1,0:T(8,128)(2,1)S(1)}, bf16[1024,1536]{1,0:T(8,128)(2,1)}, f32[1536,1536]{1,0:T(8,128)}) %tuple.294), branch_computations={%region_19.20_spmd, %region_20.21_spmd} | conditional | flops 1210713088 | bytes 20449102 | solution.py:39
  219.6 9.2 %convolution_add_fusion.4 = f32[1536,1536]{1,0:T(8,128)} fusion(f32[1536,1536]{1,0:T(8,128)} %get-tuple-element.467, bf16[1024,1536]{1,0:T(8,128)(2,1)} %get-tuple-element.471, s32[]{:T(128)S(6)} %select_n.177, bf16[1024,1536]{1,0:T(8,128)(2,1)S(1)} %get-tuple-element.470, pred[256]{0:T(512)(128)(4,1)S(1)} %compare_and_fusion.6), kind=kOutput, calls=%fused_computation.54 | convolution fusion | flops 1210712064 | bytes 20448768 | tf_op jit(solution)/shard_map/cond/branch_1_fun/dot_general | solution.py:24
  228.8 4.7 conditional.44
  228.8 4.7 broadcast.382
  233.8 30.7 %fusion.197 = (bf16[1536,1536]{1,0:T(8,128)(2,1)}, bf16[1536,1536]{1,0:T(8,128)(2,1)}, bf16[1536,1536]{1,0:T(8,128)(2,1)}, bf16[1536,1536]{1,0:T(8,128)(2,1)}, b...) fusion(bf16[1536,1536]{1,0:T(8,128)(2,1)} %param.58, f32[1536,1536]{1,0:T(8,128)} %get-tuple-element.758, ...), kind=kLoop, calls=%fused_computation.252 | loop fusion | flops 44826624 | bytes 89653272 | tf_op jit(solution)/shard_map/convert_element_type | solution.py:46
  264.4 192.5 %while.12 = (s32[]{:T(128)}, f32[16,192,768]{2,1,0:T(8,128)}, s32[16]{0:T(128)S(1)}, bf16[1536,1536]{1,0:T(8,128)(2,1)}, bf16[1536,256]{1,0:T(8,128)(2,1)S(1)}, ...) while((s32[]{:T(128)}, f32[16,192,768]{2,1,0:T(8,128)}, ...), condition=%wide.region_56.57_spmd, body=%wide.region_55.56_spmd.sunk | while | flops 452984864 | bytes 7668744 | solution.py:100
  375.3 1.4 convolution_dynamic-update-slice_fusion.12
  387.4 1.4 convolution_dynamic-update-slice_fusion.12
  411.5 1.4 convolution_dynamic-update-slice_fusion.12
  447.7 1.4 convolution_dynamic-update-slice_fusion.12
  457.0 201.9 %reduce-scatter.2.cloned.1.call-done = f32[192,768]{1,0:T(8,128)} async-done(((f32[3072,768]{1,0:T(8,128)}), f32[192,768]{1,0:T(8,128)}) %reduce-scatter.2.cloned.1.call-update) | async-done | bytes 589840 | tf_op jit(solution)/shard_map/reduce_scatter | solution.py:104
  (167 shorter events, 155.6 us)
Async XLA Ops:
  6.5 90.5 %copy-start.2 = (s32[6]{0:T(128)S(1)}, s32[6]{0:T(128)}, u32[]{:S(2)}) copy-start(s32[6]{0:T(128)} %param.59) | copy-start | bytes 76
  6.5 88.6 %all-gather.2.cloned.1.call-start = ((), (), s32[]{:S(2)}) async-start(), calls=%async_computation.1 | async-start | bytes 3538944 | tf_op jit(solution)/shard_map/all_gather | solution.py:67
  23.1 147.3 %all-reduce.4.cloned.1.call-start = ((), (), s32[]{:S(2)}) async-start(), calls=%async_computation.3 | async-start | bytes 7864320 | tf_op jit(solution)/shard_map/psum | solution.py:12
  95.1 75.3 %copy-start.1 = (bf16[1024,1536]{1,0:T(8,128)(2,1)S(1)}, bf16[1024,1536]{1,0:T(8,128)(2,1)}, u32[]{:S(2)}) copy-start(bf16[1024,1536]{1,0:T(8,128)(2,1)} %all-gather.2.cloned.1.call-done) | copy-start | bytes 9437188
  97.0 561.8 %reduce-scatter.2.cloned.1.call-start = ((), (), s32[]{:S(2)}) async-start(), calls=%async_computation.2 | async-start | bytes 10027008 | tf_op jit(solution)/shard_map/reduce_scatter | solution.py:104
  233.8 30.7 %copy-start = (bf16[1536,256]{1,0:T(8,128)(2,1)S(1)}, bf16[1536,256]{1,0:T(8,128)(2,1)}, u32[]{:S(2)}) copy-start(bf16[1536,256]{1,0:T(8,128)(2,1)} %get-tuple-element.677) | copy-start | bytes 2359300
Sparse Core Ops, SparseCore 0:
  23.2 71.8 all-gather.1
  97.6 72.6 all-reduce.3
  457.1 201.6 reduce-scatter.1
where the time goes:
time: 681 us; the launch traced here: 668 us
  waiting for transfers between devices  329 us (48%)
  matrix products  173 us (25%)
  local copies, waits for them, and re-layouts  44.8 us (7%)
  loops' own time  40.7 us (6%)
  other arithmetic  38.7 us (6%)
  between operations  29.1 us (4%)
  blocking collectives  12.6 us (2%)
    reduce_scatter x1, waiting for transfers between devices, shards(): lax.psum_scatter(stacked.reshape(lax.axis_size(('segment', 'col')) * dev_...  202 us
    dot_general x96, matrix products, one_piece(): jnp.dot(lax.dynamic_slice_in_dim(hadamard, block_num * dev_rows, dev_rows...  132 us
    all_gather x1, waiting for transfers between devices, shards(): row_geno = lax.all_gather(standard, 'col', axis=0, tiled=True)  71 us
    psum x1, waiting for transfers between devices, broadcast(): return lax.psum(jnp.where(mine, shard, jnp.zeros_like(shard)), axis)  56.4 us
    dot_general x5, matrix products, gram_update(): lax.dot_general(left_block, right_block, (((0,), (0,)), ((), ())), prefer...  40.3 us
    another operation x1, loops' own time, shards(): lax.map(one_piece, jnp.arange(lax.axis_size(('segment', 'col')) * dev_row...  36.9 us
    convert_element_type x1, other arithmetic, make_hadamard(): (local_gram / seg_count.astype(jnp.float32) * global_grm).astype(jnp.bflo...  30.7 us
    another operation x4, local copies, waits for them, and re-layouts  19.2 us
  transfers between devices with their start and end apart: 3, of which 3 were waited for; matrix products, arithmetic and copies ran while one was open for 0% of the time, Pallas kernels for 0%

commit v1 on v0

v1 whole, which is shorter than its diff:
```python
import functools

import jax
import jax.numpy as jnp
from jax import lax
from jax.experimental import pallas as pl
from jax.experimental.pallas import tpu as pltpu
from jax.sharding import PartitionSpec as P

MESH_ID = pl.DeviceIdType.MESH
OWN = [(0, 0, 0), (0, 0, 2), (0, 0, 1), (0, 0, 3)]
ARRIVE = [
    (0, 1, 2), (1, 0, 0), (3, 0, 1),
    (0, 1, 3), (1, 0, 2), (3, 0, 3),
    (1, 0, 1), (3, 0, 0), (0, 1, 0),
    (1, 0, 3), (3, 0, 2), (0, 1, 1),
    (2, 0, 0), (2, 0, 1), (1, 1, 0),
    (1, 1, 2), (3, 1, 3), (3, 1, 1),
    (2, 0, 2), (2, 0, 3), (1, 1, 1),
    (1, 1, 3), (3, 1, 2), (3, 1, 0),
    (2, 1, 2), (2, 1, 3), (2, 1, 0), (2, 1, 1),
]
LAGS = {1: 11, 2: 16, 3: 21}
QROWS = 384


def piece_index(piece):
    dx, dz, q = piece
    return (dx * 2 + dz) * 4 + q


def gather_kernel(dosage, missing, resid, rows_out, cols_out, res_out,
                  turned, own, stat_mine, stat_in,
                  stat_send, stat_recv, own_sem, row_send, row_recv,
                  chain_send, chip_send, col_recv, res_send, res_recv):
    seg, row, col = lax.axis_index("segment"), lax.axis_index("row"), lax.axis_index("col")
    y, core = row // 2, row % 2
    x, zl = col // 2, col % 2
    samples = dosage.shape[1]
    col_of = lambda dx, dz: lax.rem(x + 4 - dx, 4) * 2 + lax.rem(zl + dz, 2)
    right = (seg, row, lax.rem(x + 1, 4) * 2 + zl)
    left = (seg, row, lax.rem(x + 3, 4) * 2 + zl)
    across = (seg, row, x * 2 + 1 - zl)
    up = (seg, lax.rem(y + 1, 4) * 2 + core, col)
    down = (seg, lax.rem(y + 3, 4) * 2 + core, col)
    mate = (seg, y * 2 + 1 - core, col)
    carries = core == zl
    place = lax.rem(y + 4 - x, 4)
    source = carries & (place == 0)
    takes = jnp.logical_not(source)

    barrier = pltpu.get_barrier_semaphore()
    peers = [(seg, lax.rem(row + d, 8), col) for d in range(1, 8)] + [right, left, across]
    for peer in peers:
        pl.semaphore_signal(barrier, inc=1, device_id=peer, device_id_type=MESH_ID)

    def turn(j, sums):
        lanes = pl.ds(pl.multiple_of(j * 128, 128), 128)
        tile = jnp.where(missing[:, lanes] == 0, dosage[:, lanes], -1.0).T
        turned[lanes, :] = tile
        seen = (tile >= 0.0).astype(jnp.float32).reshape(16, 8, 128)
        alt = jnp.maximum(tile, 0.0).reshape(16, 8, 128)
        return sums[0] + jnp.sum(alt, axis=0), sums[1] + jnp.sum(seen, axis=0)

    zero = jnp.zeros((8, 128), jnp.float32)
    alt, seen = lax.fori_loop(0, samples // 128, turn, (zero, zero))
    which = lax.broadcasted_iota(jnp.int32, (8, 128), 0)
    stat_mine[...] = jnp.where(which == 0, jnp.sum(alt, axis=0, keepdims=True),
                               jnp.sum(seen, axis=0, keepdims=True))

    pl.semaphore_wait(barrier, len(peers))

    def res_copy(half, target, n, src):
        part = pl.ds(half * (samples // 2), samples // 2)
        return pltpu.make_async_remote_copy(
            src_ref=src.at[part], dst_ref=res_out.at[part],
            send_sem=res_send.at[n], recv_sem=res_recv.at[half],
            device_id=target, device_id_type=MESH_ID)

    def stat_copy(d):
        return pltpu.make_async_remote_copy(
            src_ref=stat_mine, dst_ref=stat_in.at[d - 1],
            send_sem=stat_send.at[d - 1], recv_sem=stat_recv.at[d - 1],
            device_id=(seg, lax.rem(row + d, 8), col), device_id_type=MESH_ID)

    for d in range(1, 8):
        stat_copy(d).start()

    @pl.when(source)
    def _():
        res_copy(0, up, 0, resid).start()
        res_copy(1, down, 1, resid).start()
        res_copy(0, mate, 2, resid).start()
        res_copy(1, mate, 3, resid).start()

    total = stat_mine[...]
    for d in range(1, 8):
        stat_copy(d).wait_recv()
        total = total + stat_in[d - 1]
    alt, seen = total[0:1], total[1:2]
    freq = (alt + 1.0) / (2.0 * seen + 2.0)
    twice = 2.0 * freq
    scale = 1.0 / jnp.sqrt(twice * (1.0 - freq))

    def piece_rows(q):
        return pl.ds(q * QROWS, QROWS)

    def row_copy(n, piece, target, rel):
        dx, dz, q = piece
        c = col_of(dx, dz)
        src = own.at[piece_rows(q)] if (dx, dz) == (0, 0) else rows_out.at[c, piece_rows(q)]
        return pltpu.make_async_remote_copy(
            src_ref=src, dst_ref=rows_out.at[c, piece_rows(q)],
            send_sem=row_send.at[n], recv_sem=row_recv.at[piece_index(rel)],
            device_id=target, device_id_type=MESH_ID)

    def row_arrival(piece):
        dx, dz, q = piece
        dst = rows_out.at[col_of(dx, dz), piece_rows(q)]
        return pltpu.make_async_remote_copy(
            src_ref=dst, dst_ref=dst, send_sem=row_send.at[0],
            recv_sem=row_recv.at[piece_index(piece)], device_id=right, device_id_type=MESH_ID)

    sends = []

    def send_row(piece, where):
        dx, dz, q = piece
        if where == "right":
            target, rel = right, ((dx + 1) % 4, dz, q)
        elif where == "left":
            target, rel = left, ((dx + 3) % 4, dz, q)
        else:
            target, rel = across, (dx, 1 - dz, q)
        copy = row_copy(len(sends), piece, target, rel)
        copy.start()
        sends.append(copy)

    def col_ref(piece):
        dx, dz, q = piece
        return cols_out.at[col_of(dx, dz), piece_rows(q)]

    def chain_copy(piece, src, q):
        return pltpu.make_async_remote_copy(
            src_ref=src, dst_ref=col_ref(piece),
            send_sem=chain_send.at[piece_index(piece)], recv_sem=col_recv.at[piece_index(piece)],
            device_id=up if q < 2 else down, device_id_type=MESH_ID)

    def chip_copy(piece, src):
        return pltpu.make_async_remote_copy(
            src_ref=src, dst_ref=col_ref(piece),
            send_sem=chip_send.at[piece_index(piece)], recv_sem=col_recv.at[piece_index(piece)],
            device_id=mate, device_id_type=MESH_ID)

    def relays(q):
        last = 3 if q < 2 else 1
        return carries & (place != 0) & (place != last)

    def from_source(piece):
        dx, dz, q = piece
        src = own.at[piece_rows(q)] if (dx, dz) == (0, 0) else rows_out.at[col_of(dx, dz), piece_rows(q)]

        @pl.when(source)
        def _():
            chain_copy(piece, src, q).start()
            chip_copy(piece, src).start()

    def pass_on(piece, here):
        q = piece[2]
        last = 3 if q < 2 else 1
        chip_copy(piece, col_ref(piece)).wait_recv()
        if here != last:
            chain_copy(piece, col_ref(piece), q).start()
        chip_copy(piece, col_ref(piece)).start()

    def pass_res(half):
        @pl.when(carries & (place != 0))
        def _():
            res_copy(half, mate, 0, res_out).wait_recv()

            @pl.when(place != (3 if half == 0 else 1))
            def _():
                res_copy(half, up if half == 0 else down, half, res_out).start()
            res_copy(half, mate, 2 + half, res_out).start()

    def standardize(q):
        def tile(t, _):
            part = pl.ds(pl.multiple_of(q * QROWS + t * 128, 128), 128)
            v = turned[part, :]
            own[part, :] = jnp.where(v >= 0.0, (v - twice) * scale, 0.0).astype(jnp.bfloat16)
            return 0
        lax.fori_loop(0, QROWS // 128, tile, 0, unroll=True)

    for piece in OWN:
        standardize(piece[2])
    for piece in OWN:
        q = piece[2]
        from_source(piece)
        send_row(piece, "right")
        send_row((0, 0, (1, 0, 3, 2)[q]), "left")
        send_row((0, 0, (2, 3, 0, 1)[q]), "across")
    keep = pltpu.make_async_copy(own, rows_out.at[col], own_sem)
    keep.start()

    order = list(OWN) + list(ARRIVE)
    pass_res(0)
    pass_res(1)

    def chain_step(t):
        for here in (1, 2, 3):
            due = []
            for hops in (1, 2, 3):
                j = t - LAGS[hops]
                if 0 <= j < len(order) and (here if order[j][2] < 2 else 4 - here) == hops:
                    due.append(order[j])
            if t == len(OWN):
                for j in range(t):
                    hops = here if order[j][2] < 2 else 4 - here
                    if j + LAGS[hops] < t:
                        due.insert(0, order[j])
            if due:
                @pl.when(carries & (place == here))
                def _(due=due, here=here):
                    for piece in due:
                        pass_on(piece, here)

    for i, piece in enumerate(ARRIVE):
        dx, dz, q = piece
        row_arrival(piece).wait_recv()
        if (dx, dz) == (0, 1) and q >= 2:
            send_row(piece, "right" if q == 2 else "left")
            send_row(piece, "left" if q == 2 else "right")
        if dx == 1 and q in (0, 2) and (dz == 0 or q == 2):
            send_row(piece, "right")
        if dx == 3 and q in (1, 3) and (dz == 0 or q == 3):
            send_row(piece, "left")
        if dz == 0 and q < 2:
            send_row(piece, "across")
        from_source(piece)
        chain_step(i + len(OWN))
    for t in range(len(order), len(order) + LAGS[3]):
        chain_step(t)

    keep.wait()
    for copy in sends:
        copy.wait_send()
    for d in range(1, 8):
        stat_copy(d).wait_send()

    @pl.when(source)
    def _():
        for half in (0, 1):
            res_copy(half, up if half == 0 else down, half, resid).wait_send()
            res_copy(half, mate, 2 + half, resid).wait_send()
        for piece in order:
            q = piece[2]
            chain_copy(piece, col_ref(piece), q).wait_send()
            chip_copy(piece, col_ref(piece)).wait_send()

    @pl.when(carries & (place != 0))
    def _():
        for half in (0, 1):
            res_copy(half, mate, 2 + half, res_out).wait_send()
        for piece in order:
            chip_copy(piece, col_ref(piece)).wait_send()

    for half in (0, 1):
        @pl.when(relays(0 if half == 0 else 2))
        def _(half=half):
            res_copy(half, up if half == 0 else down, half, res_out).wait_send()
            for piece in order:
                if (piece[2] >= 2) == (half == 1):
                    chain_copy(piece, col_ref(piece), piece[2]).wait_send()

    @pl.when(jnp.logical_not(carries))
    def _():
        for half in (0, 1):
            res_copy(half, mate, 0, res_out).wait_recv()
        for piece in order:
            chip_copy(piece, col_ref(piece)).wait_recv()


def gather(dosage, missing, residuals):
    variants, samples = dosage.shape
    tile = jax.ShapeDtypeStruct((8, samples, variants), jnp.bfloat16)
    vmem = pl.BlockSpec(memory_space=pltpu.VMEM)
    hbm = pl.BlockSpec(memory_space=pl.ANY)
    dma = pltpu.SemaphoreType.DMA
    return pl.pallas_call(
        gather_kernel,
        out_shape=(tile, tile, jax.ShapeDtypeStruct(residuals.shape, residuals.dtype)),
        in_specs=[vmem, vmem, hbm],
        out_specs=(hbm, hbm, hbm),
        scratch_shapes=[
            pltpu.VMEM((samples, variants), jnp.float32),
            pltpu.VMEM((samples, variants), jnp.bfloat16),
            pltpu.VMEM((8, 128), jnp.float32),
            pltpu.VMEM((7, 8, 128), jnp.float32),
            dma((7,)), dma((7,)), dma(()), dma((28,)), dma((32,)),
            dma((32,)), dma((32,)), dma((32,)), dma((4,)), dma((2,)),
        ],
        compiler_params=pltpu.CompilerParams(collective_id=1, has_side_effects=True),
        name="gather_genotypes",
    )(dosage, missing, residuals)


SLOTS = 5
DEPTH = 256
NT = (((1,), (1,)), ((), ()))


def scores_kernel(meta, inv, rows, rows_all, cols_all, grm, res_own, res_all, out,
                  cols, res, acc, sems):
    tiles = cols.shape[1] // 256

    @pl.when(pl.program_id(0) == 0)
    def _():
        def fetch(col_src, res_src):
            one = pltpu.make_async_copy(col_src, cols, sems.at[0])
            two = pltpu.make_async_copy(res_src, res, sems.at[1])
            one.start()
            two.start()
            one.wait()
            two.wait()

        pl.when(meta[2 * SLOTS] == 1)(lambda: fetch(rows_all, res_own))
        pl.when(meta[2 * SLOTS] == 0)(lambda: fetch(cols_all, res_all))

    def slot(k, carry):
        lower, upper = meta[2 * k], meta[2 * k + 1]
        first = lower // DEPTH
        blocks = jnp.where(upper > lower, (upper + DEPTH - 1) // DEPTH - first, 0)

        def with_blocks(count):
            left = []
            for i in range(count):
                block = jnp.concatenate(
                    [rows[2 * (first + i)], rows[2 * (first + i) + 1]], axis=1)
                variant = (first + i) * DEPTH + lax.broadcasted_iota(jnp.int32, block.shape, 1)
                keep = (variant >= lower) & (variant < upper)
                left.append(jnp.where(keep, block, jnp.zeros_like(block)))
            left = jnp.concatenate(left, axis=1)
            for t in range(tiles):
                part = pl.ds(t * 256, 256)
                right = jnp.concatenate(
                    [cols[2 * first + j, part, :] for j in range(2 * count)], axis=1)
                gram = lax.dot_general(left, right, NT, preferred_element_type=jnp.float32)
                hadamard = (gram * grm[:, part].astype(jnp.float32)).astype(jnp.bfloat16)
                term = jnp.dot(hadamard, res[part, :], preferred_element_type=jnp.float32)
                if t == 0:
                    acc[...] = term
                else:
                    acc[...] += term
            total = (acc[...] * inv[k]).astype(jnp.bfloat16)
            for j in range(out.shape[1]):
                for half in range(2):
                    out[half, j, k] = total[j * 192:(j + 1) * 192, half * 128:(half + 1) * 128]

        for count in range(1, 5):
            pl.when(blocks == count)(functools.partial(with_blocks, count))

        @pl.when(blocks == 0)
        def _():
            for j in range(out.shape[1]):
                for half in range(2):
                    out[half, j, k] = jnp.zeros((192, 128), out.dtype)

        return carry

    lax.fori_loop(0, SLOTS, slot, 0)


def local_scores(meta, inv, rows, cols, grm, res_own, res_all, step=768):
    samples = rows.shape[1]
    hbm = pl.BlockSpec(memory_space=pl.ANY)
    return pl.pallas_call(
        scores_kernel,
        out_shape=jax.ShapeDtypeStruct((2, 8, SLOTS, 192, 128), jnp.bfloat16),
        grid_spec=pltpu.PrefetchScalarGridSpec(
            num_scalar_prefetch=2, grid=(samples // step,),
            in_specs=[
                pl.BlockSpec((8, step, 128), lambda m, *_: (0, m, 0)),
                hbm, hbm,
                pl.BlockSpec((step, samples), lambda m, *_: (m, 0)),
                hbm, hbm,
            ],
            out_specs=pl.BlockSpec((2, step // 192, SLOTS, 192, 128), lambda m, *_: (0, m, 0, 0, 0)),
            scratch_shapes=[
                pltpu.VMEM((8, samples, 128), jnp.bfloat16),
                pltpu.VMEM(res_own.shape, res_own.dtype),
                pltpu.VMEM((step, 256), jnp.float32),
                pltpu.SemaphoreType.DMA((2,)),
            ],
        ),
        compiler_params=pltpu.CompilerParams(vmem_limit_bytes=60 << 20),
        name="local_scores",
    )(meta, inv, rows, rows, cols, grm, res_own, res_all)


SEGS = 6


def scatter_kernel(parts, out, from_x, from_z, mid_x, mid_z, last_z, last_x,
                   own_sem, one_send, one_recv, two_send, two_recv):
    seg, row, col = lax.axis_index("segment"), lax.axis_index("row"), lax.axis_index("col")
    x, zl = col // 2, col % 2
    z = seg * 2 + zl
    rows = out.shape[1] // 2
    top, low = pl.ds(0, rows), pl.ds(rows, rows)

    def at(to_x, to_z):
        return (to_z // 2, row, to_x * 2 + to_z % 2)

    def shifted(base, d):
        return lax.rem(base + d, 4)

    barrier = pltpu.get_barrier_semaphore()
    for d in (1, 2, 3):
        pl.semaphore_signal(barrier, inc=1, device_id=at(shifted(x, d), z), device_id_type=MESH_ID)
        pl.semaphore_signal(barrier, inc=1, device_id=at(x, shifted(z, d)), device_id_type=MESH_ID)
    pl.semaphore_wait(barrier, 6)

    def x_one(d, j):
        to_x, for_z = shifted(x, d), shifted(z, j)
        return pltpu.make_async_remote_copy(
            src_ref=parts.at[for_z // 2, to_x, for_z % 2, :, top],
            dst_ref=from_x.at[j % 4, x],
            send_sem=one_send.at[0, d - 1, j - 1], recv_sem=one_recv.at[0, d - 1, j - 1],
            device_id=at(to_x, z), device_id_type=MESH_ID)

    def z_one(d, j):
        to_z, for_x = shifted(z, d), shifted(x, j)
        return pltpu.make_async_remote_copy(
            src_ref=parts.at[to_z // 2, for_x, to_z % 2, :, low],
            dst_ref=from_z.at[j % 4, z],
            send_sem=one_send.at[1, d - 1, j - 1], recv_sem=one_recv.at[1, d - 1, j - 1],
            device_id=at(x, to_z), device_id_type=MESH_ID)

    def own_copy(axis, j):
        if axis == 0:
            for_z = shifted(z, j)
            src, dst = parts.at[for_z // 2, x, for_z % 2, :, top], from_x.at[j % 4, x]
        else:
            for_x = shifted(x, j)
            src, dst = parts.at[z // 2, for_x, z % 2, :, low], from_z.at[j % 4, z]
        return pltpu.make_async_copy(src, dst, own_sem.at[axis, j - 1])

    def x_two(j):
        to_z = shifted(z, j)
        return pltpu.make_async_remote_copy(
            src_ref=mid_x.at[j - 1], dst_ref=last_z.at[z],
            send_sem=two_send.at[0, j - 1], recv_sem=two_recv.at[0, j - 1],
            device_id=at(x, to_z), device_id_type=MESH_ID)

    def z_two(j):
        to_x = shifted(x, j)
        return pltpu.make_async_remote_copy(
            src_ref=mid_z.at[j - 1], dst_ref=last_x.at[x],
            send_sem=two_send.at[1, j - 1], recv_sem=two_recv.at[1, j - 1],
            device_id=at(to_x, z), device_id_type=MESH_ID)

    order = (2, 1, 3, 4)
    for j in order:
        own_copy(0, j).start()
        own_copy(1, j).start()
        for d in (2, 1, 3):
            x_one(d, j).start()
            z_one(d, j).start()

    f32 = jnp.float32
    for j in order:
        own_copy(0, j).wait()
        for d in (1, 2, 3):
            x_one(d, j).wait_recv()
        for k in range(SLOTS):
            got = [from_x[j % 4, i, k].astype(f32) for i in range(4)]
            total = ((got[0] + got[1]) + (got[2] + got[3])).astype(jnp.bfloat16)
            if j < 4:
                mid_x[j - 1, k] = total
            else:
                last_z[z, k] = total
        if j < 4:
            x_two(j).start()
        own_copy(1, j).wait()
        for d in (1, 2, 3):
            z_one(d, j).wait_recv()
        for s in range(SEGS):
            total = jnp.zeros((rows, 128), f32)
            if s < SLOTS:
                total = from_z[j % 4, 0, s].astype(f32) + from_z[j % 4, 1, s].astype(f32)
            if s > 0:
                total = total + (from_z[j % 4, 2, s - 1].astype(f32) + from_z[j % 4, 3, s - 1].astype(f32))
            total = total.astype(jnp.bfloat16)
            if j < 4:
                mid_z[j - 1, s] = total
            else:
                last_x[x, s] = total
        if j < 4:
            z_two(j).start()

    for j in (1, 2, 3):
        x_two(j).wait_recv()
        z_two(j).wait_recv()
    for s in range(SEGS):
        total = jnp.zeros((rows, 128), f32)
        if s < SLOTS:
            total = last_z[0, s].astype(f32) + last_z[1, s].astype(f32)
        if s > 0:
            total = total + (last_z[2, s - 1].astype(f32) + last_z[3, s - 1].astype(f32))
        out[s, top] = total.astype(jnp.bfloat16)
        got = [last_x[i, s].astype(f32) for i in range(4)]
        out[s, low] = ((got[0] + got[1]) + (got[2] + got[3])).astype(jnp.bfloat16)

    for j in order:
        for d in (1, 2, 3):
            x_one(d, j).wait_send()
            z_one(d, j).wait_send()
        if j < 4:
            x_two(j).wait_send()
            z_two(j).wait_send()


def scatter(parts):
    rows, lanes = parts.shape[-2:]
    parts = parts.reshape(2, 4, 2, SLOTS, rows, lanes)
    half = rows // 2
    bf16 = jnp.bfloat16
    dma = pltpu.SemaphoreType.DMA
    return pl.pallas_call(
        scatter_kernel,
        out_shape=jax.ShapeDtypeStruct((SEGS, rows, lanes), bf16),
        in_specs=[pl.BlockSpec(memory_space=pl.ANY)],
        out_specs=pl.BlockSpec(memory_space=pltpu.VMEM),
        scratch_shapes=[
            pltpu.VMEM((4, 4, SLOTS, half, lanes), bf16),
            pltpu.VMEM((4, 4, SLOTS, half, lanes), bf16),
            pltpu.VMEM((3, SLOTS, half, lanes), bf16),
            pltpu.VMEM((3, SEGS, half, lanes), bf16),
            pltpu.VMEM((4, SLOTS, half, lanes), bf16),
            pltpu.VMEM((4, SEGS, half, lanes), bf16),
            dma((2, 4)), dma((2, 3, 4)), dma((2, 3, 4)), dma((2, 3)), dma((2, 3)),
        ],
        compiler_params=pltpu.CompilerParams(collective_id=2, has_side_effects=True),
        name="scatter_scores",
    )(parts)


def shards(dosage, missing, residuals, global_grm, seg_counts):
    seg, row, col = lax.axis_index("segment"), lax.axis_index("row"), lax.axis_index("col")
    shard_vars = 8 * dosage.shape[0]
    ends = jnp.cumsum(seg_counts) - seg * shard_vars
    starts = ends - seg_counts
    near = lambda v: lax.dynamic_slice_in_dim(v, seg, SLOTS, 0)
    lower = near(jnp.clip(starts, 0, shard_vars))
    upper = near(jnp.clip(ends, 0, shard_vars))
    bounds = jnp.stack([lower, upper], axis=1).reshape(-1)
    meta = jnp.concatenate([bounds, (row == col).astype(jnp.int32)[None]]).astype(jnp.int32)
    inv = 1.0 / near(seg_counts).astype(jnp.float32)
    rows, cols, res = gather(dosage, missing, residuals)
    parts = local_scores(meta, inv, rows, cols, global_grm, residuals, res)
    return scatter(parts)


def solution(mesh):
    placed = (
        P(("segment", "col"), "row"),
        P(("segment", "col"), "row"),
        P("row", None),
        P("row", "col"),
        P(),
    )
    return jax.shard_map(
        shards,
        mesh=mesh,
        in_specs=placed,
        out_specs=P(None, ("row", "col"), "segment"),
        check_vma=False,
    )
```

time: 681 us -> 146 us (0.21); the launches traced: 668 us -> 144 us
  waiting for transfers between devices: 329 us -> 0 us
  matrix products: 173 us -> 0 us
  Pallas kernels: 0 us -> 138 us
  local copies, waits for them, and re-layouts: 44.8 us -> 1.95 us
  loops' own time: 40.7 us -> 0 us
  other arithmetic: 38.7 us -> 3.41 us
  between operations: 29.1 us -> 0.03 us
  blocking collectives: 12.6 us -> 0 us
    reduce_scatter x1 -> x0, waiting for transfers between devices: 202 us -> none  [shards(): lax.psum_scatter(stacked.reshape(lax.axis_size(('segment', 'col')) * dev_...]
    dot_general x101 -> x0, matrix products: 173 us -> none  [the longest x96 132 us: one_piece(): jnp.dot(lax.dynamic_slice_in_dim(hadamard, block_num * dev_rows, dev_rows...]
    pallas_call x0 -> x3, Pallas kernels: none -> 138 us  [the longest x1 78.3 us: gather(): pl.pallas_call(gather_kernel, out_shape=(tile, tile, jax.ShapeDtypeStruct...]
    all_gather x1 -> x0, waiting for transfers between devices: 71 us -> none  [shards(): row_geno = lax.all_gather(standard, 'col', axis=0, tiled=True)]
    psum x1 -> x0, waiting for transfers between devices: 56.4 us -> none  [broadcast(): return lax.psum(jnp.where(mine, shard, jnp.zeros_like(shard)), axis)]
    another operation x25 -> x0, loops' own time: 40.7 us -> none  [the longest x1 36.9 us: shards(): lax.map(one_piece, jnp.arange(lax.axis_size(('segment', 'col')) * dev_row...]
    convert_element_type x3 -> x0, other arithmetic: 34.1 us -> none  [the longest x1 30.7 us: make_hadamard(): (local_gram / seg_count.astype(jnp.float32) * global_grm).astype(jnp.bflo...]
    another operation x4 -> x2, local copies, waits for them, and re-layouts: 19.2 us -> 0.17 us  [shards(): bounds = jnp.stack([lower, upper], axis=1).reshape(-1)]
  transfers between devices with their start and end apart: 3 -> 0, of which waited for: 3 -> 0; matrix products, arithmetic and copies ran while one was open for 0% -> 0% of each run, Pallas kernels for 0% -> 0%
where the time goes in v1:
time: 146 us; the launch traced here: 144 us
  Pallas kernels  138 us (95%)
  other arithmetic  3.41 us (2%)
  local copies, waits for them, and re-layouts  1.95 us (1%)
    pallas_call x1, Pallas kernels, gather(): pl.pallas_call(gather_kernel, out_shape=(tile, tile, jax.ShapeDtypeStruct...  78.3 us
    pallas_call x1, Pallas kernels, scatter(): pl.pallas_call(scatter_kernel, out_shape=jax.ShapeDtypeStruct((SEGS, rows...  42.5 us
    pallas_call x1, Pallas kernels, local_scores(): pl.pallas_call(scores_kernel, out_shape=jax.ShapeDtypeStruct((2, 8, SLOTS...  17.5 us

profile of v1, /device:TPU:3, one launch (start us, length us, event | category | flops | bytes accessed | tf_op | source)
XLA Modules:
  0.0 143.7 jit_solution(11818276862396690157)
XLA Ops:
  0.0 0.8 reduce-window.9
  0.8 0.7 fusion
  1.5 0.1 dynamic-slice_bitcast_fusion
  1.6 1.3 convert_divide_fusion.inv
  2.9 0.1 copy.7
  3.0 0.1 reshape.33
  3.1 0.6 pad_add_fusion.1.meta
  3.7 78.3 %gather_genotypes.1 = (bf16[8,1536,128]{2,1,0:T(8,128)(2,1)}, bf16[8,1536,128]{2,1,0:T(8,128)(2,1)}, bf16[1536,256]{1,0:T(8,128)(2,1)}) custom-call(f32[128,1536]{1,0:T(8,128)} %dosage.1, s32[128,1536]{1,0:T(8,128)} %missing.1, bf16[1536,256]{1,0:T(8,128)(2,1)} %res_own.1), custom_call_target="tpu_custom_call" | custom-call | tf_op jit(solution)/shard_map/gather_genotypes/pallas_call | solution.py:288
  82.0 17.5 %local_scores.1 = bf16[2,8,5,192,128]{4,3,2,1,0:T(8,128)(2,1)} custom-call(s32[11]{0:T(128)} %pad_add_fusion.1.meta, f32[5]{0:T(128)} %convert_divide_fusion.inv, bf16[8,1536,128]{2,1,0:T(8,128)(2,1)} %get-tuple-element.8.rows.rows_all, bf16[8,1536,128]{2,1,0:T(8,128)(2,1)} %get-tuple-element.8.rows.rows_all, ...), custom_call_target="tpu_custom_call" | custom-call | tf_op jit(solution)/shard_map/local_scores/pallas_call | solution.py:375
  99.5 42.5 %scatter_scores.1 = bf16[6,192,128]{2,1,0:T(8,128)(2,1)} custom-call(bf16[2,4,2,5,192,128]{5,4,3,2,1,0:T(8,128)(2,1)} %bitcast.12), custom_call_target="tpu_custom_call" | custom-call | tf_op jit(solution)/shard_map/scatter_scores/pallas_call | solution.py:528
  142.0 1.7 %copy.9 = bf16[6,192,128]{2,1,0:T(8,128)(2,1)} copy(bf16[6,192,128]{2,1,0:T(8,128)(2,1)} %scatter_scores.1) | data formatting | bytes 589824
  (1 shorter events, 0.0 us)

commit v2 on v0

v2 whole, which is shorter than its diff:
```python
import functools

import jax
import jax.numpy as jnp
from jax import lax
from jax.experimental import pallas as pl
from jax.experimental.pallas import tpu as pltpu
from jax.sharding import PartitionSpec as P

MESH_ID = pl.DeviceIdType.MESH
OWN = [(0, 0, 0), (0, 0, 2), (0, 0, 1), (0, 0, 3)]
ARRIVE = [
    (0, 1, 2), (1, 0, 0), (3, 0, 1),
    (0, 1, 3), (1, 0, 2), (3, 0, 3),
    (1, 0, 1), (3, 0, 0), (0, 1, 0),
    (1, 0, 3), (3, 0, 2), (0, 1, 1),
    (2, 0, 0), (2, 0, 1), (1, 1, 0),
    (1, 1, 2), (3, 1, 3), (3, 1, 1),
    (2, 0, 2), (2, 0, 3), (1, 1, 1),
    (1, 1, 3), (3, 1, 2), (3, 1, 0),
    (2, 1, 2), (2, 1, 3), (2, 1, 0), (2, 1, 1),
]
LAGS = {0: 4, 1: 12, 2: 18, 3: 24}
RES_AT = (-8, -8, -6, -6)
QROWS = 384


RES = [(4, 0, 0), (4, 0, 2), (4, 0, 1), (4, 0, 3)]


def piece_index(piece):
    dx, dz, q = piece
    return (dx * 2 + dz) * 4 + q


def gather_kernel(dosage, missing, resid, rows_out, cols_out, res_out,
                  turned, own, stat_mine, stat_in,
                  stat_send, stat_recv, own_sem, row_send, row_recv,
                  chain_send, chip_send, col_recv):
    seg, row, col = lax.axis_index("segment"), lax.axis_index("row"), lax.axis_index("col")
    y, core = row // 2, row % 2
    x, zl = col // 2, col % 2
    samples = dosage.shape[1]
    col_of = lambda dx, dz: lax.rem(x + 4 - dx, 4) * 2 + lax.rem(zl + dz, 2)
    right = (seg, row, lax.rem(x + 1, 4) * 2 + zl)
    left = (seg, row, lax.rem(x + 3, 4) * 2 + zl)
    across = (seg, row, x * 2 + 1 - zl)
    up = (seg, lax.rem(y + 1, 4) * 2 + core, col)
    down = (seg, lax.rem(y + 3, 4) * 2 + core, col)
    mate = (seg, y * 2 + 1 - core, col)
    first = core == zl
    place = lax.rem(y + 4 - x, 4)
    source = first & (place == 0)
    helper = jnp.logical_not(first) & (place == 0)

    barrier = pltpu.get_barrier_semaphore()
    peers = [(seg, lax.rem(row + d, 8), col) for d in range(1, 8)] + [right, left, across]
    for peer in peers:
        pl.semaphore_signal(barrier, inc=1, device_id=peer, device_id_type=MESH_ID)

    def turn(j, sums):
        lanes = pl.ds(pl.multiple_of(j * 128, 128), 128)
        tile = jnp.where(missing[:, lanes] == 0, dosage[:, lanes], -1.0).T
        turned[lanes, :] = tile
        seen = (tile >= 0.0).astype(jnp.float32).reshape(16, 8, 128)
        alt = jnp.maximum(tile, 0.0).reshape(16, 8, 128)
        return sums[0] + jnp.sum(alt, axis=0), sums[1] + jnp.sum(seen, axis=0)

    zero = jnp.zeros((8, 128), jnp.float32)
    alt, seen = lax.fori_loop(0, samples // 128, turn, (zero, zero))
    which = lax.broadcasted_iota(jnp.int32, (8, 128), 0)
    stat_mine[...] = jnp.where(which == 0, jnp.sum(alt, axis=0, keepdims=True),
                               jnp.sum(seen, axis=0, keepdims=True))

    pl.semaphore_wait(barrier, len(peers))

    def piece_rows(q):
        return pl.ds(q * QROWS, QROWS)

    def col_ref(piece):
        dx, dz, q = piece
        if dx == 4:
            return res_out.at[piece_rows(q)]
        return cols_out.at[col_of(dx, dz), piece_rows(q)]

    def chain_copy(piece, src, q):
        return pltpu.make_async_remote_copy(
            src_ref=src, dst_ref=col_ref(piece),
            send_sem=chain_send.at[piece_index(piece)], recv_sem=col_recv.at[piece_index(piece)],
            device_id=up if q < 2 else down, device_id_type=MESH_ID)

    def chip_copy(piece, src):
        return pltpu.make_async_remote_copy(
            src_ref=src, dst_ref=col_ref(piece),
            send_sem=chip_send.at[piece_index(piece)], recv_sem=col_recv.at[piece_index(piece)],
            device_id=mate, device_id_type=MESH_ID)

    def from_source(piece):
        dx, dz, q = piece
        if dx == 4:
            src = resid.at[piece_rows(q)]
        else:
            here = (dx, dz) == (0, 0)
            src = own.at[piece_rows(q)] if here else rows_out.at[col_of(dx, dz), piece_rows(q)]

        @pl.when(source)
        def _():
            chip_copy(piece, src).start()
            if q % 2 == 0:
                chain_copy(piece, src, q).start()

    def stat_copy(d):
        return pltpu.make_async_remote_copy(
            src_ref=stat_mine, dst_ref=stat_in.at[d - 1],
            send_sem=stat_send.at[d - 1], recv_sem=stat_recv.at[d - 1],
            device_id=(seg, lax.rem(row + d, 8), col), device_id_type=MESH_ID)

    for d in range(1, 8):
        stat_copy(d).start()

    for piece in RES:
        from_source(piece)

    total = stat_mine[...]
    for d in range(1, 8):
        stat_copy(d).wait_recv()
        total = total + stat_in[d - 1]
    alt, seen = total[0:1], total[1:2]
    freq = (alt + 1.0) / (2.0 * seen + 2.0)
    twice = 2.0 * freq
    scale = 1.0 / jnp.sqrt(twice * (1.0 - freq))

    def row_copy(n, piece, target, rel):
        dx, dz, q = piece
        c = col_of(dx, dz)
        src = own.at[piece_rows(q)] if (dx, dz) == (0, 0) else rows_out.at[c, piece_rows(q)]
        return pltpu.make_async_remote_copy(
            src_ref=src, dst_ref=rows_out.at[c, piece_rows(q)],
            send_sem=row_send.at[n], recv_sem=row_recv.at[piece_index(rel)],
            device_id=target, device_id_type=MESH_ID)

    def row_arrival(piece):
        dx, dz, q = piece
        dst = rows_out.at[col_of(dx, dz), piece_rows(q)]
        return pltpu.make_async_remote_copy(
            src_ref=dst, dst_ref=dst, send_sem=row_send.at[0],
            recv_sem=row_recv.at[piece_index(piece)], device_id=right, device_id_type=MESH_ID)

    sends = []

    def send_row(piece, where):
        dx, dz, q = piece
        if where == "right":
            target, rel = right, ((dx + 1) % 4, dz, q)
        elif where == "left":
            target, rel = left, ((dx + 3) % 4, dz, q)
        else:
            target, rel = across, (dx, 1 - dz, q)
        copy = row_copy(len(sends), piece, target, rel)
        copy.start()
        sends.append(copy)

    def carrier(q):
        return first if q % 2 == 0 else jnp.logical_not(first)

    def pass_on(piece, here):
        q = piece[2]
        last = 3 if q < 2 else 1
        chip_copy(piece, col_ref(piece)).wait_recv()
        if here != last:
            chain_copy(piece, col_ref(piece), q).start()
        if here != 0:
            chip_copy(piece, col_ref(piece)).start()

    def standardize(q):
        def tile(t, _):
            part = pl.ds(pl.multiple_of(q * QROWS + t * 128, 128), 128)
            v = turned[part, :]
            own[part, :] = jnp.where(v >= 0.0, (v - twice) * scale, 0.0).astype(jnp.bfloat16)
            return 0
        lax.fori_loop(0, QROWS // 128, tile, 0, unroll=True)

    for piece in OWN:
        standardize(piece[2])
    for piece in OWN:
        q = piece[2]
        from_source(piece)
        send_row(piece, "right")
        send_row((0, 0, (1, 0, 3, 2)[q]), "left")
        send_row((0, 0, (2, 3, 0, 1)[q]), "across")
    keep = pltpu.make_async_copy(own, rows_out.at[col], own_sem)
    keep.start()

    order = RES + OWN + ARRIVE
    timed = list(zip(RES_AT, RES)) + list(enumerate(OWN + ARRIVE))

    def chain_step(t):
        for parity in (0, 1):
            for here in (0, 1, 2, 3):
                due = []
                for j, piece in timed:
                    if piece[2] % 2 != parity or (here == 0 and parity == 0):
                        continue
                    hops = here if piece[2] < 2 else (4 - here) % 4
                    if max(j + LAGS[hops], len(OWN)) == t:
                        due.append(piece)
                if due:
                    @pl.when(carrier(parity) & (place == here))
                    def _(due=due, here=here):
                        for piece in due:
                            pass_on(piece, here)

    for i, piece in enumerate(ARRIVE):
        dx, dz, q = piece
        row_arrival(piece).wait_recv()
        if (dx, dz) == (0, 1) and q >= 2:
            send_row(piece, "right" if q == 2 else "left")
            send_row(piece, "left" if q == 2 else "right")
        if dx == 1 and q in (0, 2) and (dz == 0 or q == 2):
            send_row(piece, "right")
        if dx == 3 and q in (1, 3) and (dz == 0 or q == 3):
            send_row(piece, "left")
        if dz == 0 and q < 2:
            send_row(piece, "across")
        from_source(piece)
        chain_step(i + len(OWN))
    for t in range(len(OWN + ARRIVE), len(OWN + ARRIVE) + LAGS[3]):
        chain_step(t)

    keep.wait()
    for copy in sends:
        copy.wait_send()
    for d in range(1, 8):
        stat_copy(d).wait_send()

    @pl.when(source)
    def _():
        for piece in order:
            chip_copy(piece, col_ref(piece)).wait_send()
            if piece[2] % 2 == 0:
                chain_copy(piece, col_ref(piece), piece[2]).wait_send()

    @pl.when(helper)
    def _():
        for piece in order:
            if piece[2] % 2 == 0:
                chip_copy(piece, col_ref(piece)).wait_recv()
            else:
                chain_copy(piece, col_ref(piece), piece[2]).wait_send()

    for q in range(4):
        mine = [piece for piece in order if piece[2] == q]
        last = 3 if q < 2 else 1

        @pl.when(carrier(q) & (place != 0))
        def _(mine=mine):
            for piece in mine:
                chip_copy(piece, col_ref(piece)).wait_send()

        @pl.when(carrier(q) & (place != 0) & (place != last))
        def _(mine=mine):
            for piece in mine:
                chain_copy(piece, col_ref(piece), piece[2]).wait_send()

        @pl.when(jnp.logical_not(carrier(q)) & (place != 0))
        def _(mine=mine):
            for piece in mine:
                chip_copy(piece, col_ref(piece)).wait_recv()


def gather(dosage, missing, residuals):
    variants, samples = dosage.shape
    tile = jax.ShapeDtypeStruct((8, samples, variants), jnp.bfloat16)
    vmem = pl.BlockSpec(memory_space=pltpu.VMEM)
    hbm = pl.BlockSpec(memory_space=pl.ANY)
    dma = pltpu.SemaphoreType.DMA
    return pl.pallas_call(
        gather_kernel,
        out_shape=(tile, tile, jax.ShapeDtypeStruct(residuals.shape, residuals.dtype)),
        in_specs=[vmem, vmem, hbm],
        out_specs=(hbm, hbm, hbm),
        scratch_shapes=[
            pltpu.VMEM((samples, variants), jnp.float32),
            pltpu.VMEM((samples, variants), jnp.bfloat16),
            pltpu.VMEM((8, 128), jnp.float32),
            pltpu.VMEM((7, 8, 128), jnp.float32),
            dma((7,)), dma((7,)), dma(()), dma((28,)), dma((32,)),
            dma((36,)), dma((36,)), dma((36,)),
        ],
        compiler_params=pltpu.CompilerParams(collective_id=1, has_side_effects=True),
        name="gather_genotypes",
    )(dosage, missing, residuals)


SLOTS = 5
SEGS = 6
DEPTH = 256
STEPS = 8
XO = (2, 1, 3, 0)


def scores_kernel(counts, rows_all, cols_all, grm_all, res_own, res_all, out,
                  rows, cols, wide, grm, res, acc, parts, from_x, from_z, mid_x, mid_z, last_z, last_x,
                  plan, load_sem, one_send, one_recv, two_send, two_recv):
    seg, row, col = (lax.axis_index(a) for a in ("segment", "row", "col"))
    x, zl = col // 2, col % 2
    z = seg * 2 + zl
    f32, bf16 = jnp.float32, jnp.bfloat16
    samples = cols.shape[1]
    shard = cols.shape[0] * cols.shape[2]
    chunk = samples // 4
    half = out.shape[1] // 2
    top, low = pl.ds(0, half), pl.ds(half, half)

    def at(to_x, to_z):
        return (to_z // 2, row, to_x * 2 + to_z % 2)

    def shifted(base, d):
        return lax.rem(base + d, 4)

    barrier = pltpu.get_barrier_semaphore()
    for d in (1, 2, 3):
        pl.semaphore_signal(barrier, inc=1, device_id=at(shifted(x, d), z), device_id_type=MESH_ID)
        pl.semaphore_signal(barrier, inc=1, device_id=at(x, shifted(z, d)), device_id_type=MESH_ID)

    def load(n, src, dst):
        return pltpu.make_async_copy(src, dst, load_sem.at[n])

    def chunk_rows(t):
        return pl.ds(pl.multiple_of(shifted(x, XO[t]) * chunk, chunk), chunk)

    def row_load(t):
        return load(2 + t, rows_all.at[:, chunk_rows(t)], rows.at[t])

    def grm_load(t):
        return load(6 + t, grm_all.at[chunk_rows(t)], grm.at[t])

    diagonal = row == col

    @pl.when(diagonal)
    def _():
        load(0, rows_all, cols).start()
        load(1, res_own, res).start()

    @pl.when(jnp.logical_not(diagonal))
    def _():
        load(0, cols_all, cols).start()
        load(1, res_all, res).start()

    for t in range(4):
        row_load(t).start()
        grm_load(t).start()

    flip = seg == 1
    sizes = [jnp.where(flip, counts[SEGS - 1 - i], counts[i]) for i in range(SLOTS)]
    ends, total = [], jnp.int32(0)
    for size in sizes:
        total = total + size
        ends.append(jnp.minimum(total, shard))
    pos, k = jnp.int32(0), jnp.int32(0)
    for j in range(STEPS):
        end, size = ends[SLOTS - 1], sizes[SLOTS - 1]
        for i in range(SLOTS - 2, -1, -1):
            end = jnp.where(k <= i, ends[i], end)
            size = jnp.where(k <= i, sizes[i], size)
        block = jnp.minimum(pos // DEPTH, shard // DEPTH - 1)
        stop = jnp.maximum(jnp.minimum(end, (block + 1) * DEPTH), pos)
        plan[0, j] = jnp.where(flip, shard // DEPTH - 1 - block, block)
        plan[1, j] = jnp.where(flip, shard - stop, pos)
        plan[2, j] = jnp.where(flip, shard - pos, stop)
        plan[3, j] = k
        plan[4, j] = size
        k = jnp.where(stop == end, k + 1, k)
        pos = stop

    load(0, cols_all, cols).wait()

    def widen(b, carry):
        wide[b, 0:128, :] = cols[2 * b].T
        wide[b, 128:256, :] = cols[2 * b + 1].T
        return carry

    lax.fori_loop(0, shard // DEPTH, widen, 0)
    load(1, res_all, res).wait()
    for t in range(4):
        row_load(t).wait()
    pl.semaphore_wait(barrier, 6)

    def compute(t, carry):
        acc[...] = jnp.zeros_like(acc)
        for j in range(STEPS):
            block, lower, upper = plan[0, j], plan[1, j], plan[2, j]
            left = jnp.concatenate([rows[t, 2 * block], rows[t, 2 * block + 1]], axis=1)
            variant = block * DEPTH + lax.broadcasted_iota(jnp.int32, left.shape, 1)
            left = jnp.where((variant >= lower) & (variant < upper), left, jnp.zeros_like(left))
            term = None
            for n in range(samples // 256):
                part = pl.ds(n * 256, 256)
                gram = jnp.dot(left, wide[block, :, part], preferred_element_type=f32)
                hadamard = (gram * grm[t, :, part].astype(f32)).astype(bf16)
                new = jnp.dot(hadamard, res[part, :], preferred_element_type=f32)
                term = new if term is None else term + new
            scale = 1.0 / jnp.full((1, 256), plan[4, j], jnp.int32).astype(f32)
            term = term * scale
            for k in range(max(0, j - 3), min(j, SLOTS - 1) + 1):
                acc[k] += jnp.where(plan[3, j] == k, term, 0.0)
        for k in range(SLOTS):
            for i in range(4):
                r = (i % 2) * 2 * half
                lanes = slice((i // 2) * 128, (i // 2) * 128 + 128)
                parts[t, i, k] = acc[k, r:r + 2 * half, lanes].astype(bf16)
        return carry

    def x_one(t, i):
        return pltpu.make_async_remote_copy(
            src_ref=parts.at[t, i, :, top], dst_ref=from_x.at[i, t],
            send_sem=one_send.at[0, t, i], recv_sem=one_recv.at[0, t, i],
            device_id=at(shifted(x, XO[t]), z), device_id_type=MESH_ID)

    def z_one(t, d):
        to_z = shifted(z, d)
        return pltpu.make_async_remote_copy(
            src_ref=parts.at[t, to_z, :, low], dst_ref=from_z.at[t, d - 1],
            send_sem=one_send.at[1, t, d], recv_sem=one_recv.at[1, t, d],
            device_id=at(x, to_z), device_id_type=MESH_ID)

    def x_two(d):
        to_z = shifted(z, d)
        return pltpu.make_async_remote_copy(
            src_ref=mid_x.at[to_z], dst_ref=last_z.at[d - 1],
            send_sem=two_send.at[0, d], recv_sem=two_recv.at[0, d],
            device_id=at(x, to_z), device_id_type=MESH_ID)

    def z_two(t):
        return pltpu.make_async_remote_copy(
            src_ref=mid_z.at[t], dst_ref=last_x.at[t],
            send_sem=two_send.at[1, t], recv_sem=two_recv.at[1, t],
            device_id=at(shifted(x, XO[t]), z), device_id_type=MESH_ID)

    def place_slots(write, mine, others):
        def go(near, far, seg_is):
            for s in range(SEGS):
                total = jnp.zeros((half, 128), f32)
                i = s if seg_is == 0 else SEGS - 1 - s
                if i < SLOTS:
                    total = total + (mine(i) + others(near, i))
                if SEGS - 1 - i < SLOTS:
                    total = total + (others(far, SEGS - 1 - i) + others(2, SEGS - 1 - i))
                write(s, total)

        for seg_is in (0, 1):
            for zl_is in (0, 1):
                near, far = (3, 1) if zl_is == 0 else (1, 3)

                @pl.when((seg == seg_is) & (zl == zl_is))
                def _(near=near, far=far, seg_is=seg_is):
                    go(near, far, seg_is)

    def low_sum(t):
        for d in (1, 2, 3):
            z_one(t, d).wait_recv()

        def write(s, total):
            mid_z[t, s] = total.astype(bf16)

        place_slots(write, lambda i: parts[t, z, i, low, :].astype(f32),
                    lambda d, i: from_z[t, d - 1, i].astype(f32))
        if XO[t] != 0:
            z_two(t).start()

    for t in range(4):
        grm_load(t).wait()
        compute(t, 0)
        for i in (1, 2, 3, 0):
            if XO[t] != 0:
                x_one(t, i).start()
        for d in (2, 1, 3):
            z_one(t, d).start()
        if t > 0:
            low_sum(t - 1)

    def top_sum(i):
        for t in range(3):
            x_one(t, i).wait_recv()
        for k in range(SLOTS):
            got = [from_x[i, t, k].astype(f32) for t in range(3)]
            total = (got[0] + got[1]) + (got[2] + parts[3, i, k, top, :].astype(f32))
            mid_x[i, k] = total.astype(bf16)

    for i in range(4):
        top_sum(i)
    for d in (2, 1, 3):
        x_two(d).start()
    low_sum(3)
    for t in range(3):
        z_two(t).wait_recv()
    for s in range(SEGS):
        got = [last_x[t, s].astype(f32) for t in range(3)]
        out[s, low] = ((got[0] + got[1]) + (got[2] + mid_z[3, s].astype(f32))).astype(bf16)
    for d in (1, 2, 3):
        x_two(d).wait_recv()

    def write(s, total):
        out[s, top] = total.astype(bf16)

    place_slots(write, lambda i: mid_x[z, i].astype(f32), lambda d, i: last_z[d - 1, i].astype(f32))

    for t in range(4):
        if XO[t] != 0:
            for i in range(4):
                x_one(t, i).wait_send()
            z_two(t).wait_send()
        for d in (1, 2, 3):
            z_one(t, d).wait_send()
    for d in (1, 2, 3):
        x_two(d).wait_send()


def scores(seg_counts, rows, cols, grm, res_own, res_all):
    samples = rows.shape[1]
    out_rows = samples // 8
    half = out_rows // 2
    bf16 = jnp.bfloat16
    dma = pltpu.SemaphoreType.DMA
    hbm = pl.BlockSpec(memory_space=pl.ANY)
    return pl.pallas_call(
        scores_kernel,
        out_shape=jax.ShapeDtypeStruct((SEGS, out_rows, 128), bf16),
        in_specs=[pl.BlockSpec(memory_space=pltpu.SMEM), hbm, hbm, hbm, hbm, hbm],
        out_specs=pl.BlockSpec(memory_space=pltpu.VMEM),
        scratch_shapes=[
            pltpu.VMEM((4, 8, samples // 4, 128), bf16),
            pltpu.VMEM((8, samples, 128), bf16),
            pltpu.VMEM((4, DEPTH, samples), bf16),
            pltpu.VMEM((4, samples // 4, samples), bf16),
            pltpu.VMEM(res_own.shape, bf16),
            pltpu.VMEM((SLOTS, samples // 4, 256), jnp.float32),
            pltpu.VMEM((4, 4, SLOTS, out_rows, 128), bf16),
            pltpu.VMEM((4, 3, SLOTS, half, 128), bf16),
            pltpu.VMEM((4, 3, SLOTS, half, 128), bf16),
            pltpu.VMEM((4, SLOTS, half, 128), bf16),
            pltpu.VMEM((4, SEGS, half, 128), bf16),
            pltpu.VMEM((3, SLOTS, half, 128), bf16),
            pltpu.VMEM((3, SEGS, half, 128), bf16),
            pltpu.SMEM((5, STEPS), jnp.int32),
            dma((10,)), dma((2, 4, 4)), dma((2, 4, 4)), dma((2, 4)), dma((2, 4)),
        ],
        compiler_params=pltpu.CompilerParams(
            vmem_limit_bytes=60 << 20, collective_id=2, has_side_effects=True),
        name="scores",
    )(seg_counts, rows, cols, grm, res_own, res_all)


def shards(dosage, missing, residuals, global_grm, seg_counts):
    rows, cols, res = gather(dosage, missing, residuals)
    return scores(seg_counts, rows, cols, global_grm, residuals, res)


def solution(mesh):
    placed = (
        P(("segment", "col"), "row"),
        P(("segment", "col"), "row"),
        P("row", None),
        P("row", "col"),
        P(),
    )
    return jax.shard_map(
        shards,
        mesh=mesh,
        in_specs=placed,
        out_specs=P(None, ("row", "col"), "segment"),
        check_vma=False,
    )
```

time: 681 us -> 106 us (0.16); the launches traced: 668 us -> 105 us
  waiting for transfers between devices: 329 us -> 0 us
  matrix products: 173 us -> 0 us
  Pallas kernels: 0 us -> 103 us
  local copies, waits for them, and re-layouts: 44.8 us -> 1.69 us
  loops' own time: 40.7 us -> 0 us
  other arithmetic: 38.7 us -> 0 us
  between operations: 29.1 us -> 0.02 us
  blocking collectives: 12.6 us -> 0 us
    reduce_scatter x1 -> x0, waiting for transfers between devices: 202 us -> none  [shards(): lax.psum_scatter(stacked.reshape(lax.axis_size(('segment', 'col')) * dev_...]
    dot_general x101 -> x0, matrix products: 173 us -> none  [the longest x96 132 us: one_piece(): jnp.dot(lax.dynamic_slice_in_dim(hadamard, block_num * dev_rows, dev_rows...]
    pallas_call x0 -> x2, Pallas kernels: none -> 103 us  [the longest x1 55.2 us: gather(): pl.pallas_call(gather_kernel, out_shape=(tile, tile, jax.ShapeDtypeStruct...]
    all_gather x1 -> x0, waiting for transfers between devices: 71 us -> none  [shards(): row_geno = lax.all_gather(standard, 'col', axis=0, tiled=True)]
    psum x1 -> x0, waiting for transfers between devices: 56.4 us -> none  [broadcast(): return lax.psum(jnp.where(mine, shard, jnp.zeros_like(shard)), axis)]
    another operation x25 -> x0, loops' own time: 40.7 us -> none  [the longest x1 36.9 us: shards(): lax.map(one_piece, jnp.arange(lax.axis_size(('segment', 'col')) * dev_row...]
    convert_element_type x3 -> x0, other arithmetic: 34.1 us -> none  [the longest x1 30.7 us: make_hadamard(): (local_gram / seg_count.astype(jnp.float32) * global_grm).astype(jnp.bflo...]
    another operation x4 -> x0, local copies, waits for them, and re-layouts: 19.2 us -> none
  transfers between devices with their start and end apart: 3 -> 0, of which waited for: 3 -> 0; matrix products, arithmetic and copies ran while one was open for 0% -> 0% of each run, Pallas kernels for 0% -> 0%
where the time goes in v2:
time: 106 us; the launch traced here: 105 us
  Pallas kernels  103 us (97%)
  local copies, waits for them, and re-layouts  1.69 us (2%)
    pallas_call x1, Pallas kernels, gather(): pl.pallas_call(gather_kernel, out_shape=(tile, tile, jax.ShapeDtypeStruct...  55.2 us
    pallas_call x1, Pallas kernels, scores(): pl.pallas_call(scores_kernel, out_shape=jax.ShapeDtypeStruct((SEGS, out_r...  48.1 us

profile of v2, /device:TPU:3, one launch (start us, length us, event | category | flops | bytes accessed | tf_op | source)
XLA Modules:
  0.0 105.1 jit_solution(1417068350914551417)
XLA Ops:
  0.0 55.2 %gather_genotypes.1 = (bf16[8,1536,128]{2,1,0:T(8,128)(2,1)}, bf16[8,1536,128]{2,1,0:T(8,128)(2,1)}, bf16[1536,256]{1,0:T(8,128)(2,1)}) custom-call(f32[128,1536]{1,0:T(8,128)} %dosage.1, s32[128,1536]{1,0:T(8,128)} %missing.1, bf16[1536,256]{1,0:T(8,128)(2,1)} %res_own.1), custom_call_target="tpu_custom_call" | custom-call | tf_op jit(solution)/shard_map/gather_genotypes/pallas_call | solution.py:277
  55.2 48.1 %scores.1 = bf16[6,192,128]{2,1,0:T(8,128)(2,1)} custom-call(s32[6]{0:T(128)} %counts.1, bf16[8,1536,128]{2,1,0:T(8,128)(2,1)} %get-tuple-element.8.rows_all, bf16[8,1536,128]{2,1,0:T(8,128)(2,1)} %get-tuple-element.9.cols_all, bf16[1536,1536]{1,0:T(8,128)(2,1)} %grm_all.1, bf16[1536,256]{1,0:T(8,128)(2,1)} %res_own.1, ...), custom_call_target="tpu_custom_call" | custom-call | tf_op jit(solution)/shard_map/scores/pallas_call | solution.py:526
  103.4 1.7 %copy.7 = bf16[6,192,128]{2,1,0:T(8,128)(2,1)} copy(bf16[6,192,128]{2,1,0:T(8,128)(2,1)} %scores.1) | data formatting | bytes 589824

commit v3 on v2

--- a/solution.py
+++ b/solution.py
@@ -10,18 +10,49 @@
 MESH_ID = pl.DeviceIdType.MESH
 OWN = [(0, 0, 0), (0, 0, 2), (0, 0, 1), (0, 0, 3)]
 ARRIVE = [
-    (0, 1, 2), (1, 0, 0), (3, 0, 1),
-    (0, 1, 3), (1, 0, 2), (3, 0, 3),
-    (1, 0, 1), (3, 0, 0), (0, 1, 0),
-    (1, 0, 3), (3, 0, 2), (0, 1, 1),
-    (2, 0, 0), (2, 0, 1), (1, 1, 0),
-    (1, 1, 2), (3, 1, 3), (3, 1, 1),
-    (2, 0, 2), (2, 0, 3), (1, 1, 1),
-    (1, 1, 3), (3, 1, 2), (3, 1, 0),
-    (2, 1, 2), (2, 1, 3), (2, 1, 0), (2, 1, 1),
+    (0, 1, 2), (1, 0, 0), (3, 0, 1), (1, 0, 2), (3, 0, 3), (0, 1, 0),
+    (0, 1, 3), (1, 0, 1), (3, 0, 0), (1, 0, 3), (3, 0, 2), (0, 1, 1),
+    (1, 1, 0), (1, 1, 2), (3, 1, 2), (2, 0, 0), (2, 0, 1), (3, 1, 1),
+    (2, 0, 2), (2, 0, 3), (1, 1, 1), (3, 1, 0), (3, 1, 3), (1, 1, 3),
+    (2, 1, 2), (2, 1, 0), (2, 1, 1), (2, 1, 3),
 ]
-LAGS = {0: 4, 1: 12, 2: 18, 3: 24}
-RES_AT = (-8, -8, -6, -6)
+CHAIN = {
+    (0, 1): [
+        (4, 4, 0, 1), (4, 4, 0, 3), (4, 0, 0, 1), (4, 0, 0, 3), (6, 3, 0, 1), (9, 3, 0, 3),
+        (12, 0, 1, 3), (12, 1, 0, 1), (15, 1, 0, 3), (15, 0, 1, 1), (21, 3, 1, 1), (21, 2, 0, 1),
+        (25, 2, 0, 3), (27, 1, 1, 1), (27, 3, 1, 3), (27, 1, 1, 3), (31, 2, 1, 1), (31, 2, 1, 3),
+    ],
+    (1, 0): [
+        (4, 4, 0, 0), (4, 0, 0, 0), (12, 1, 0, 0), (18, 0, 1, 0), (21, 3, 0, 0), (21, 4, 0, 2),
+        (21, 0, 0, 2), (25, 1, 1, 0), (27, 2, 0, 0), (27, 0, 1, 2), (30, 3, 1, 0), (31, 1, 0, 2),
+        (31, 2, 1, 0), (31, 3, 0, 2), (31, 1, 1, 2), (31, 3, 1, 2), (31, 2, 0, 2), (31, 2, 1, 2),
+    ],
+    (1, 1): [
+        (12, 4, 0, 1), (15, 0, 0, 1), (15, 3, 0, 1), (21, 1, 0, 1), (23, 0, 1, 1), (27, 3, 1, 1),
+        (28, 4, 0, 3), (29, 2, 0, 1), (29, 0, 0, 3), (30, 3, 0, 3), (31, 1, 1, 1), (31, 0, 1, 3),
+        (31, 1, 0, 3), (31, 2, 1, 1), (31, 2, 0, 3), (31, 3, 1, 3), (31, 1, 1, 3), (31, 2, 1, 3),
+    ],
+    (2, 0): [
+        (12, 4, 0, 0), (12, 4, 0, 2), (15, 0, 0, 0), (15, 0, 0, 2), (21, 0, 1, 2), (21, 1, 0, 0),
+        (24, 1, 0, 2), (25, 0, 1, 0), (27, 3, 0, 0), (28, 3, 0, 2), (31, 2, 0, 0), (31, 3, 1, 2),
+        (31, 1, 1, 0), (31, 1, 1, 2), (31, 2, 0, 2), (31, 3, 1, 0), (31, 2, 1, 0), (31, 2, 1, 2),
+    ],
+    (2, 1): [
+        (21, 4, 0, 1), (21, 4, 0, 3), (21, 0, 0, 1), (21, 0, 0, 3), (25, 3, 0, 1), (27, 3, 0, 3),
+        (27, 0, 1, 3), (29, 1, 0, 1), (30, 1, 0, 3), (31, 0, 1, 1), (31, 3, 1, 1), (31, 2, 0, 3),
+        (31, 2, 0, 1), (31, 3, 1, 3), (31, 1, 1, 1), (31, 1, 1, 3), (31, 2, 1, 1), (31, 2, 1, 3),
+    ],
+    (3, 0): [
+        (4, 4, 0, 2), (4, 0, 0, 2), (12, 0, 1, 2), (15, 1, 0, 2), (21, 4, 0, 0), (21, 3, 0, 2),
+        (21, 0, 0, 0), (25, 1, 1, 2), (27, 3, 1, 2), (27, 1, 0, 0), (29, 2, 0, 2), (31, 0, 1, 0),
+        (31, 3, 0, 0), (31, 2, 1, 2), (31, 2, 0, 0), (31, 1, 1, 0), (31, 3, 1, 0), (31, 2, 1, 0),
+    ],
+    (3, 1): [
+        (12, 4, 0, 3), (15, 0, 0, 3), (18, 3, 0, 3), (21, 0, 1, 3), (23, 1, 0, 3), (28, 4, 0, 1),
+        (29, 0, 0, 1), (30, 2, 0, 3), (31, 3, 0, 1), (31, 3, 1, 3), (31, 1, 1, 3), (31, 1, 0, 1),
+        (31, 0, 1, 1), (31, 2, 1, 3), (31, 3, 1, 1), (31, 2, 0, 1), (31, 1, 1, 1), (31, 2, 1, 1),
+    ],
+}
 QROWS = 384
 
 
@@ -192,23 +223,15 @@
     keep.start()
 
     order = RES + OWN + ARRIVE
-    timed = list(zip(RES_AT, RES)) + list(enumerate(OWN + ARRIVE))
 
     def chain_step(t):
-        for parity in (0, 1):
-            for here in (0, 1, 2, 3):
-                due = []
-                for j, piece in timed:
-                    if piece[2] % 2 != parity or (here == 0 and parity == 0):
-                        continue
-                    hops = here if piece[2] < 2 else (4 - here) % 4
-                    if max(j + LAGS[hops], len(OWN)) == t:
-                        due.append(piece)
-                if due:
-                    @pl.when(carrier(parity) & (place == here))
-                    def _(due=due, here=here):
-                        for piece in due:
-                            pass_on(piece, here)
+        for (here, parity), steps in CHAIN.items():
+            due = [tuple(entry[1:]) for entry in steps if entry[0] == t]
+            if due:
+                @pl.when(carrier(parity) & (place == here))
+                def _(due=due, here=here):
+                    for piece in due:
+                        pass_on(piece, here)
 
     for i, piece in enumerate(ARRIVE):
         dx, dz, q = piece
@@ -224,8 +247,6 @@
             send_row(piece, "across")
         from_source(piece)
         chain_step(i + len(OWN))
-    for t in range(len(OWN + ARRIVE), len(OWN + ARRIVE) + LAGS[3]):
-        chain_step(t)
 
     keep.wait()
     for copy in sends:

time: 106 us -> 99.8 us (0.942)
  Pallas kernels: 103 us -> 97.9 us
    pallas_call x1, Pallas kernels: 55.2 us -> 49.5 us  [gather(): pl.pallas_call(gather_kernel, out_shape=(tile, tile, jax.ShapeDtypeStruct...]
where the time goes in v3:
time: 99.8 us; the launch traced here: 99.6 us
  Pallas kernels  97.9 us (98%)
  local copies, waits for them, and re-layouts  1.69 us (2%)
    pallas_call x1, Pallas kernels, gather(): pl.pallas_call(gather_kernel, out_shape=(tile, tile, jax.ShapeDtypeStruct...  49.5 us
    pallas_call x1, Pallas kernels, scores(): pl.pallas_call(scores_kernel, out_shape=jax.ShapeDtypeStruct((SEGS, out_r...  48.4 us

profile of v3, /device:TPU:3, one launch (start us, length us, event | category | flops | bytes accessed | tf_op | source)
XLA Modules:
  0.0 99.6 jit_solution(16269581270649060819)
XLA Ops:
  0.0 49.5 %gather_genotypes.1 = (bf16[8,1536,128]{2,1,0:T(8,128)(2,1)}, bf16[8,1536,128]{2,1,0:T(8,128)(2,1)}, bf16[1536,256]{1,0:T(8,128)(2,1)}) custom-call(f32[128,1536]{1,0:T(8,128)} %dosage.1, s32[128,1536]{1,0:T(8,128)} %missing.1, bf16[1536,256]{1,0:T(8,128)(2,1)} %res_own.1), custom_call_target="tpu_custom_call" | custom-call | tf_op jit(solution)/shard_map/gather_genotypes/pallas_call | solution.py:298
  49.5 48.4 %scores.1 = bf16[6,192,128]{2,1,0:T(8,128)(2,1)} custom-call(s32[6]{0:T(128)} %counts.1, bf16[8,1536,128]{2,1,0:T(8,128)(2,1)} %get-tuple-element.8.rows_all, bf16[8,1536,128]{2,1,0:T(8,128)(2,1)} %get-tuple-element.9.cols_all, bf16[1536,1536]{1,0:T(8,128)(2,1)} %grm_all.1, bf16[1536,256]{1,0:T(8,128)(2,1)} %res_own.1, ...), custom_call_target="tpu_custom_call" | custom-call | tf_op jit(solution)/shard_map/scores/pallas_call | solution.py:547
  97.9 1.7 %copy.7 = bf16[6,192,128]{2,1,0:T(8,128)(2,1)} copy(bf16[6,192,128]{2,1,0:T(8,128)(2,1)} %scores.1) | data formatting | bytes 589824

commit v4 on v3

--- a/solution.py
+++ b/solution.py
@@ -25,17 +25,17 @@
     (1, 0): [
         (4, 4, 0, 0), (4, 0, 0, 0), (12, 1, 0, 0), (18, 0, 1, 0), (21, 3, 0, 0), (21, 4, 0, 2),
         (21, 0, 0, 2), (25, 1, 1, 0), (27, 2, 0, 0), (27, 0, 1, 2), (30, 3, 1, 0), (31, 1, 0, 2),
-        (31, 2, 1, 0), (31, 3, 0, 2), (31, 1, 1, 2), (31, 3, 1, 2), (31, 2, 0, 2), (31, 2, 1, 2),
+        (31, 2, 1, 2), (31, 3, 0, 2), (31, 2, 1, 0), (31, 1, 1, 2), (31, 3, 1, 2), (31, 2, 0, 2),
     ],
     (1, 1): [
         (12, 4, 0, 1), (15, 0, 0, 1), (15, 3, 0, 1), (21, 1, 0, 1), (23, 0, 1, 1), (27, 3, 1, 1),
-        (28, 4, 0, 3), (29, 2, 0, 1), (29, 0, 0, 3), (30, 3, 0, 3), (31, 1, 1, 1), (31, 0, 1, 3),
-        (31, 1, 0, 3), (31, 2, 1, 1), (31, 2, 0, 3), (31, 3, 1, 3), (31, 1, 1, 3), (31, 2, 1, 3),
+        (28, 4, 0, 3), (29, 2, 0, 1), (29, 0, 0, 3), (30, 3, 0, 3), (31, 1, 1, 1), (31, 1, 1, 3),
+        (31, 0, 1, 3), (31, 1, 0, 3), (31, 2, 1, 1), (31, 2, 1, 3), (31, 2, 0, 3), (31, 3, 1, 3),
     ],
     (2, 0): [
         (12, 4, 0, 0), (12, 4, 0, 2), (15, 0, 0, 0), (15, 0, 0, 2), (21, 0, 1, 2), (21, 1, 0, 0),
         (24, 1, 0, 2), (25, 0, 1, 0), (27, 3, 0, 0), (28, 3, 0, 2), (31, 2, 0, 0), (31, 3, 1, 2),
-        (31, 1, 1, 0), (31, 1, 1, 2), (31, 2, 0, 2), (31, 3, 1, 0), (31, 2, 1, 0), (31, 2, 1, 2),
+        (31, 1, 1, 0), (31, 1, 1, 2), (31, 2, 0, 2), (31, 3, 1, 0), (31, 2, 1, 2), (31, 2, 1, 0),
     ],
     (2, 1): [
         (21, 4, 0, 1), (21, 4, 0, 3), (21, 0, 0, 1), (21, 0, 0, 3), (25, 3, 0, 1), (27, 3, 0, 3),
@@ -44,15 +44,16 @@
     ],
     (3, 0): [
         (4, 4, 0, 2), (4, 0, 0, 2), (12, 0, 1, 2), (15, 1, 0, 2), (21, 4, 0, 0), (21, 3, 0, 2),
-        (21, 0, 0, 0), (25, 1, 1, 2), (27, 3, 1, 2), (27, 1, 0, 0), (29, 2, 0, 2), (31, 0, 1, 0),
-        (31, 3, 0, 0), (31, 2, 1, 2), (31, 2, 0, 0), (31, 1, 1, 0), (31, 3, 1, 0), (31, 2, 1, 0),
+        (21, 0, 0, 0), (25, 1, 1, 2), (27, 3, 1, 2), (27, 1, 0, 0), (29, 2, 0, 2), (30, 3, 1, 0),
+        (31, 0, 1, 0), (31, 3, 0, 0), (31, 2, 1, 2), (31, 2, 1, 0), (31, 2, 0, 0), (31, 1, 1, 0),
     ],
     (3, 1): [
         (12, 4, 0, 3), (15, 0, 0, 3), (18, 3, 0, 3), (21, 0, 1, 3), (23, 1, 0, 3), (28, 4, 0, 1),
         (29, 0, 0, 1), (30, 2, 0, 3), (31, 3, 0, 1), (31, 3, 1, 3), (31, 1, 1, 3), (31, 1, 0, 1),
-        (31, 0, 1, 1), (31, 2, 1, 3), (31, 3, 1, 1), (31, 2, 0, 1), (31, 1, 1, 1), (31, 2, 1, 1),
+        (31, 0, 1, 1), (31, 2, 1, 1), (31, 2, 1, 3), (31, 3, 1, 1), (31, 2, 0, 1), (31, 1, 1, 1),
     ],
 }
+BOTH = [(1, 1, 3), (2, 1, 0), (2, 1, 1), (2, 1, 2), (2, 1, 3), (3, 1, 0)]
 QROWS = 384
 
 
@@ -67,7 +68,7 @@
 def gather_kernel(dosage, missing, resid, rows_out, cols_out, res_out,
                   turned, own, stat_mine, stat_in,
                   stat_send, stat_recv, own_sem, row_send, row_recv,
-                  chain_send, chip_send, col_recv):
+                  chain_send, chip_send, other_send, col_recv):
     seg, row, col = lax.axis_index("segment"), lax.axis_index("row"), lax.axis_index("col")
     y, core = row // 2, row % 2
     x, zl = col // 2, col % 2
@@ -120,6 +121,16 @@
             send_sem=chain_send.at[piece_index(piece)], recv_sem=col_recv.at[piece_index(piece)],
             device_id=up if q < 2 else down, device_id_type=MESH_ID)
 
+    def other_copy(piece, src):
+        return pltpu.make_async_remote_copy(
+            src_ref=src, dst_ref=col_ref(piece),
+            send_sem=other_send.at[BOTH.index(piece)], recv_sem=col_recv.at[piece_index(piece)],
+            device_id=down if piece[2] < 2 else up, device_id_type=MESH_ID)
+
+    def relays(piece, here):
+        near = 1 if piece[2] < 2 else 3
+        return here in ((0, near) if piece in BOTH else (0, near, 2))
+
     def chip_copy(piece, src):
         return pltpu.make_async_remote_copy(
             src_ref=src, dst_ref=col_ref(piece),
@@ -139,6 +150,8 @@
             chip_copy(piece, src).start()
             if q % 2 == 0:
                 chain_copy(piece, src, q).start()
+                if piece in BOTH:
+                    other_copy(piece, src).start()
 
     def stat_copy(d):
         return pltpu.make_async_remote_copy(
@@ -196,10 +209,11 @@
 
     def pass_on(piece, here):
         q = piece[2]
-        last = 3 if q < 2 else 1
         chip_copy(piece, col_ref(piece)).wait_recv()
-        if here != last:
+        if relays(piece, here):
             chain_copy(piece, col_ref(piece), q).start()
+        if here == 0 and piece in BOTH:
+            other_copy(piece, col_ref(piece)).start()
         if here != 0:
             chip_copy(piece, col_ref(piece)).start()
 
@@ -260,6 +274,8 @@
             chip_copy(piece, col_ref(piece)).wait_send()
             if piece[2] % 2 == 0:
                 chain_copy(piece, col_ref(piece), piece[2]).wait_send()
+                if piece in BOTH:
+                    other_copy(piece, col_ref(piece)).wait_send()
 
     @pl.when(helper)
     def _():
@@ -268,20 +284,22 @@
                 chip_copy(piece, col_ref(piece)).wait_recv()
             else:
                 chain_copy(piece, col_ref(piece), piece[2]).wait_send()
+                if piece in BOTH:
+                    other_copy(piece, col_ref(piece)).wait_send()
 
     for q in range(4):
         mine = [piece for piece in order if piece[2] == q]
-        last = 3 if q < 2 else 1
-
         @pl.when(carrier(q) & (place != 0))
         def _(mine=mine):
             for piece in mine:
                 chip_copy(piece, col_ref(piece)).wait_send()
 
-        @pl.when(carrier(q) & (place != 0) & (place != last))
-        def _(mine=mine):
-            for piece in mine:
-                chain_copy(piece, col_ref(piece), piece[2]).wait_send()
+        for here in (1, 2, 3):
+            @pl.when(carrier(q) & (place == here))
+            def _(mine=mine, here=here):
+                for piece in mine:
+                    if relays(piece, here):
+                        chain_copy(piece, col_ref(piece), piece[2]).wait_send()
 
         @pl.when(jnp.logical_not(carrier(q)) & (place != 0))
         def _(mine=mine):
@@ -306,7 +324,7 @@
             pltpu.VMEM((8, 128), jnp.float32),
             pltpu.VMEM((7, 8, 128), jnp.float32),
             dma((7,)), dma((7,)), dma(()), dma((28,)), dma((32,)),
-            dma((36,)), dma((36,)), dma((36,)),
+            dma((36,)), dma((36,)), dma((len(BOTH),)), dma((36,)),
         ],
         compiler_params=pltpu.CompilerParams(collective_id=1, has_side_effects=True),
         name="gather_genotypes",

time: 99.8 us -> 97 us (0.972)
  Pallas kernels: 97.9 us -> 95.2 us
    pallas_call x1, Pallas kernels: 49.5 us -> 46.4 us  [gather(): pl.pallas_call(gather_kernel, out_shape=(tile, tile, jax.ShapeDtypeStruct...]
where the time goes in v4:
time: 97 us; the launch traced here: 96.9 us
  Pallas kernels  95.2 us (98%)
  local copies, waits for them, and re-layouts  1.69 us (2%)
    pallas_call x1, Pallas kernels, scores(): pl.pallas_call(scores_kernel, out_shape=jax.ShapeDtypeStruct((SEGS, out_r...  48.7 us
    pallas_call x1, Pallas kernels, gather(): pl.pallas_call(gather_kernel, out_shape=(tile, tile, jax.ShapeDtypeStruct...  46.4 us

profile of v4, /device:TPU:3, one launch (start us, length us, event | category | flops | bytes accessed | tf_op | source)
XLA Modules:
  0.0 96.9 jit_solution(2229680681663644155)
XLA Ops:
  0.0 46.4 %gather_genotypes.1 = (bf16[8,1536,128]{2,1,0:T(8,128)(2,1)}, bf16[8,1536,128]{2,1,0:T(8,128)(2,1)}, bf16[1536,256]{1,0:T(8,128)(2,1)}) custom-call(f32[128,1536]{1,0:T(8,128)} %dosage.1, s32[128,1536]{1,0:T(8,128)} %missing.1, bf16[1536,256]{1,0:T(8,128)(2,1)} %res_own.1), custom_call_target="tpu_custom_call" | custom-call | tf_op jit(solution)/shard_map/gather_genotypes/pallas_call | solution.py:316
  46.4 48.7 %scores.1 = bf16[6,192,128]{2,1,0:T(8,128)(2,1)} custom-call(s32[6]{0:T(128)} %counts.1, bf16[8,1536,128]{2,1,0:T(8,128)(2,1)} %get-tuple-element.8.rows_all, bf16[8,1536,128]{2,1,0:T(8,128)(2,1)} %get-tuple-element.9.cols_all, bf16[1536,1536]{1,0:T(8,128)(2,1)} %grm_all.1, bf16[1536,256]{1,0:T(8,128)(2,1)} %res_own.1, ...), custom_call_target="tpu_custom_call" | custom-call | tf_op jit(solution)/shard_map/scores/pallas_call | solution.py:565
  95.2 1.7 %copy.7 = bf16[6,192,128]{2,1,0:T(8,128)(2,1)} copy(bf16[6,192,128]{2,1,0:T(8,128)(2,1)} %scores.1) | data formatting | bytes 589824
